TPU v7x, 256 devices: a whole 4x4x8 slice. The times are simulated.
256 devices in a mesh: seq: 64 (over y, x, z_hi, core), fsdp: 4 (over z_lo).
Axes of the slice: x: 4, y: 4, z: 8 (z_hi: 2, z_lo: 4; z = z_hi * 4 + z_lo), core: 2. Of those that a mesh axis runs over, the one named last changes fastest.
Arguments:
- tokens: bfloat16 [40960, 5120], P('seq', 'fsdp'), may hold values from -24 to 24
- w_local: bfloat16 [5120, 3, 1536], P('seq', None, 'fsdp'), may hold values from -0.078125 to 0.078125
- w_strided: bfloat16 [5120, 3, 1024], P('seq', None, 'fsdp'), may hold values from -0.078125 to 0.078125
- valid: int32 [64, 640], P('seq'), may hold values 0 or 1
- band_reach: int32 [12], P('fsdp'), may hold values from 1 to 4, as said below
Outputs:
- out_local: bfloat16 [40960, 1536], P('seq', 'fsdp')
- out_strided: bfloat16 [40960, 1024], P('seq', 'fsdp')
Inputs may be any that keep to these rules, and one draw needn't show every extreme that they name: Query block b of local head h sees band blocks b - band_reach[h] to b.
All inputs are finite; a program needn't handle non-finite values. No bound on the sum of `valid` on one device may be relied on, other than what follows from the above.
Results may differ from a plain program's by a relative error of at most 0.012.
The roundings to bfloat16 on the way count: a program that leaves them out, or rounds other values in their place, can miss the bound.
Values may be sent and summed in bfloat16 or wider, within the bound.
No kernel may reach another device: no remote copies, remote signals or barrier semaphores. Data moves between devices by JAX's collectives and lax.ppermute only.
A program may use at most 128 MiB of HBM per device.

v0:
```python
import math
import jax
import jax.numpy as jnp
from jax import lax
from jax.sharding import PartitionSpec as P

HD = 128
BLK = 128


def local_attend(qkv_day, valid_day, reach, head_size):
    query = qkv_day[:, 0]
    keys = qkv_day[:, 1]
    values = qkv_day[:, 2]
    seconds = qkv_day.shape[0]
    scores = jnp.einsum(
        "qhc,khc->hqk", query, keys, preferred_element_type=jnp.float32
    ) / math.sqrt(head_size)
    position = jnp.arange(seconds)
    causal = position[None, :] <= position[:, None]
    block = position // BLK
    band = block[None, None, :] >= block[None, :, None] - reach[:, None, None]
    seen = (valid_day[None, :] > 0) | (position[None, :] == position[:, None])
    allowed = causal[None] & band & seen[None]
    scores = jnp.where(allowed, scores, -jnp.inf)
    row_max = jnp.max(scores, axis=-1, keepdims=True)
    expo = jnp.exp(scores - row_max)
    probs = (expo / jnp.sum(expo, axis=-1, keepdims=True)).astype(jnp.bfloat16)
    result = jnp.einsum("hqk,khc->qhc", probs, values, preferred_element_type=jnp.float32)
    return result.astype(jnp.bfloat16).reshape(seconds, -1)


def body(tokens, w_local, w_strided, valid, band_reach):
    gathered = lax.all_gather(tokens, "fsdp", axis=1, tiled=True)
    seconds = gathered.shape[0]
    local_cols = w_local.shape[2]
    strided_cols = w_strided.shape[2]
    head_size = HD
    peers = lax.axis_size("seq")
    per_peer = seconds // peers

    def add_rows(piece):
        rows = piece.shape[0]
        return jnp.dot(gathered, piece.reshape(rows, -1), preferred_element_type=jnp.float32)

    acc_local = add_rows(lax.all_gather(w_local, "seq", axis=0, tiled=True))
    acc_strided = add_rows(lax.all_gather(w_strided, "seq", axis=0, tiled=True))
    packed = acc_strided.astype(jnp.bfloat16).reshape(1, peers, per_peer, 3 * strided_cols)
    marks = valid.astype(jnp.bfloat16).reshape(1, peers, per_peer)
    strided_packed = lax.all_to_all(packed, "seq", split_axis=1, concat_axis=0, tiled=True)
    strided_marks = lax.all_to_all(marks, "seq", split_axis=1, concat_axis=0, tiled=True)
    days = strided_packed.shape[0]
    count = strided_packed.shape[2]
    heads = strided_cols // head_size
    split_up = strided_packed.reshape(days, count, 3, heads, head_size)
    query = split_up[:, :, 0]
    keys = split_up[:, :, 1]
    values = split_up[:, :, 2]
    scores = jnp.einsum(
        "dshc,eshc->shde", query, keys, preferred_element_type=jnp.float32
    ) / math.sqrt(head_size)
    day = jnp.arange(days)
    causal = day[None, :] <= day[:, None]
    same = day[None, :] == day[:, None]
    seen = jnp.transpose(strided_marks[:, 0, :]) > 0
    allowed = causal[None, None] & (seen[:, None, None, :] | same[None, None])
    scores = jnp.where(allowed, scores, -jnp.inf)
    row_max = jnp.max(scores, axis=-1, keepdims=True)
    expo = jnp.exp(scores - row_max)
    probs = (expo / jnp.sum(expo, axis=-1, keepdims=True)).astype(jnp.bfloat16)
    result = jnp.einsum("shde,eshc->dshc", probs, values, preferred_element_type=jnp.float32)
    result = result.astype(jnp.bfloat16).reshape(days, 1, count, strided_cols)
    result = lax.all_to_all(result, "seq", split_axis=0, concat_axis=1, tiled=True)
    out_strided = result.reshape(seconds, strided_cols)
    qkv_local = acc_local.astype(jnp.bfloat16).reshape(
        seconds, 3, local_cols // head_size, head_size
    )
    out_local = local_attend(qkv_local, valid[0], band_reach, head_size)
    return (out_local, out_strided)


def solution(mesh):
    in_specs = (
        P("seq", "fsdp"),
        P("seq", None, "fsdp"),
        P("seq", None, "fsdp"),
        P("seq", None),
        P("fsdp"),
    )
    out_specs = (P("seq", "fsdp"), P("seq", "fsdp"))
    return jax.shard_map(body, mesh=mesh, in_specs=in_specs, out_specs=out_specs, check_vma=False)
```

profile of v0, /device:TPU:1, one launch (start us, length us, event | category | flops | bytes accessed | tf_op | source)
XLA Modules:
  0.0 441.7 jit_solution(410772100073191428)
XLA Ops:
  7.2 0.0 all-gather.8.cloned.1.call-start
  7.2 0.7 all-gather.8.cloned.1.call-update
  7.9 0.0 all-gather.4.cloned.1.call-start
  7.9 0.7 all-gather.4.cloned.1.call-update
  8.6 0.0 all-gather.6.cloned.1.call-start
  8.7 0.7 all-gather.6.cloned.1.call-update
  9.4 0.7 convert_reduce_fusion
  10.1 0.8 reshape.195
  10.9 15.6 %all-to-all-start.1 = ((bf16[1,64,10]{2,0,1:T(2,128)(2,1)}), bf16[1,64,10]{2,0,1:T(2,128)(2,1)S(1)}, u32[]{:S(2)}, u32[]{:S(2)}) async-start(bf16[1,64,10]{2,0,1:T(2,128)(2,1)} %reshape.195), calls=%async_computation.1 | async-start | bytes 65536 | tf_op jit(solution)/shard_map/all_to_all | solution.py:51
  26.5 100.5 %all-gather.8.cloned.1.call-done = bf16[5120,3,256]{2,0,1:T(8,128)(2,1)} async-done(((bf16[80,3,256]{2,0,1:T(8,128)(2,1)}), bf16[5120,3,256]{2,0,1:T(8,128)(2,1)}) %all-gather.8.cloned.1.call-update) | async-done | bytes 7864336 | tf_op jit(solution)/shard_map/all_gather | solution.py:47
  127.0 11.0 %copy.51 = bf16[5120,3,256]{0,2,1:T(8,128)(2,1)} copy(bf16[5120,3,256]{2,0,1:T(8,128)(2,1)} %all-gather.8.cloned.1.call-done) | data formatting | bytes 15728640 | tf_op jit(solution)/shard_map/all_gather | solution.py:47
  138.0 107.3 %all-gather.4.cloned.1.call-done = bf16[640,5120]{1,0:T(8,128)(2,1)} async-done(((bf16[640,1280]{1,0:T(8,128)(2,1)}), bf16[640,5120]{1,0:T(8,128)(2,1)}) %all-gather.4.cloned.1.call-update) | async-done | bytes 6553616 | tf_op jit(solution)/shard_map/all_gather | solution.py:34
  245.3 9.7 %convolution_convert_fusion.1 = bf16[640,768]{1,0:T(8,128)(2,1)S(1)} fusion(bf16[640,5120]{1,0:T(8,128)(2,1)} %all-gather.4.cloned.1.call-done, bf16[5120,768]{0,1:T(8,128)(2,1)} %bitcast.60), kind=kOutput, calls=%fused_computation.17 | convolution fusion | flops 5033656320 | bytes 15400960 | tf_op jit(solution)/shard_map/dot_general | solution.py:44
  255.0 0.0 copy-start
  255.0 1.4 reshape.189
  256.4 0.0 all-to-all-done.1
  256.4 11.4 %all-to-all-start = ((bf16[1,64,10,768]{3,2,0,1:T(8,128)(2,1)}), bf16[1,64,10,768]{3,2,0,1:T(8,128)(2,1)S(1)}, u32[]{:S(2)}, u32[]{:S(2)}) async-start(bf16[1,64,10,768]{3,2,0,1:T(8,128)(2,1)} %bitcast.8), calls=%async_computation | async-start | bytes 3145728 | tf_op jit(solution)/shard_map/all_to_all | solution.py:50
  267.9 0.0 copy-done
  267.9 0.1 copy.56
  268.0 0.2 or_and_fusion
  268.2 37.1 %all-to-all-done = bf16[1,64,10,768]{3,2,0,1:T(8,128)(2,1)S(1)} async-done(((bf16[1,64,10,768]{3,2,0,1:T(8,128)(2,1)}), bf16[1,64,10,768]{3,2,0,1:T(8,128)(2,1)S(1)}, u32[]{:S(2)}, u32[]{:S(2)}) %all-to-all-start) | async-done | bytes 983072 | tf_op jit(solution)/shard_map/all_to_all | solution.py:50
  305.3 0.6 reshape.194
  305.9 0.0 copy-start.1
  305.9 0.7 fusion.30
  306.6 0.3 fusion.14
  306.9 0.2 fusion.32
  307.1 0.3 fusion.15
  307.4 0.3 copy.69
  307.8 1.0 reshape.196
  308.8 4.4 all-to-all-start.2
  313.2 0.1 iota_compare_fusion.1
  313.3 0.0 copy-done.1
  313.3 0.1 broadcast_subtract_fusion
  313.4 0.9 fusion.10
  314.3 14.2 %all-to-all-done.2 = bf16[64,1,10,256]{3,2,1,0:T(8,128)(2,1)S(1)} async-done(((bf16[64,1,10,256]{3,2,1,0:T(8,128)(2,1)}), bf16[64,1,10,256]{3,2,1,0:T(8,128)(2,1)S(1)}, u32[]{:S(2)}, u32[]{:S(2)}) %all-to-all-start.2) | async-done | bytes 327712 | tf_op jit(solution)/shard_map/all_to_all | solution.py:73
  328.5 0.8 reshape.193
  329.4 68.7 %all-gather.6.cloned.1.call-done = bf16[5120,3,384]{2,0,1:T(8,128)(2,1)} async-done(((bf16[80,3,384]{2,0,1:T(8,128)(2,1)}), bf16[5120,3,384]{2,0,1:T(8,128)(2,1)}) %all-gather.6.cloned.1.call-update) | async-done | bytes 11796496 | tf_op jit(solution)/shard_map/all_gather | solution.py:46
  398.1 15.0 %copy.46 = bf16[5120,3,384]{0,2,1:T(8,128)(2,1)} copy(bf16[5120,3,384]{2,0,1:T(8,128)(2,1)} %all-gather.6.cloned.1.call-done) | data formatting | bytes 23592960 | tf_op jit(solution)/shard_map/all_gather | solution.py:46
  413.1 12.7 %convolution_convert_fusion = bf16[640,1152]{1,0:T(8,128)(2,1)S(1)} fusion(bf16[640,5120]{1,0:T(8,128)(2,1)} %all-gather.4.cloned.1.call-done, bf16[5120,1152]{0,1:T(8,128)(2,1)} %bitcast.59), kind=kOutput, calls=%fused_computation.5 | convolution fusion | flops 7550484480 | bytes 19824640 | tf_op jit(solution)/shard_map/dot_general | solution.py:44
  425.8 0.9 copy.47
  426.7 3.5 fusion.31
  430.2 4.0 fusion.12
  434.2 1.0 copy.62
  (4 shorter events, 0.1 us)
Async XLA Ops:
  7.2 119.8 %all-gather.8.cloned.1.call-start = ((), (), s32[]{:S(2)}) async-start(), calls=%async_computation.5 | async-start | bytes 7987200 | tf_op jit(solution)/shard_map/all_gather | solution.py:47
  7.9 237.4 %all-gather.4.cloned.1.call-start = ((), (), s32[]{:S(2)}) async-start(), calls=%async_computation.3 | async-start | bytes 8192000 | tf_op jit(solution)/shard_map/all_gather | solution.py:34
  8.6 389.4 %all-gather.6.cloned.1.call-start = ((), (), s32[]{:S(2)}) async-start(), calls=%async_computation.4 | async-start | bytes 11980800 | tf_op jit(solution)/shard_map/all_gather | solution.py:46
  10.9 245.6 %all-to-all-start.1 = ((bf16[1,64,10]{2,0,1:T(2,128)(2,1)}), bf16[1,64,10]{2,0,1:T(2,128)(2,1)S(1)}, u32[]{:S(2)}, u32[]{:S(2)}) async-start(bf16[1,64,10]{2,0,1:T(2,128)(2,1)} %reshape.195), calls=%async_computation.1 | async-start | bytes 65536 | tf_op jit(solution)/shard_map/all_to_all | solution.py:51
  255.0 12.9 %copy-start = (s32[1,640]{1,0:T(1,128)S(1)}, s32[1,640]{1,0:T(1,128)}, u32[]{:S(2)}) copy-start(s32[1,640]{1,0:T(1,128)} %param.8) | copy-start | bytes 7684
  256.4 48.9 %all-to-all-start = ((bf16[1,64,10,768]{3,2,0,1:T(8,128)(2,1)}), bf16[1,64,10,768]{3,2,0,1:T(8,128)(2,1)S(1)}, u32[]{:S(2)}, u32[]{:S(2)}) async-start(bf16[1,64,10,768]{3,2,0,1:T(8,128)(2,1)} %bitcast.8), calls=%async_computation | async-start | bytes 3145728 | tf_op jit(solution)/shard_map/all_to_all | solution.py:50
  305.9 7.4 %copy-start.1 = (s32[3]{0:T(128)S(1)}, s32[3]{0:T(128)}, u32[]{:S(2)}) copy-start(s32[3]{0:T(128)} %param.9) | copy-start | bytes 40
  308.8 19.7 %all-to-all-start.2 = ((bf16[64,1,10,256]{3,2,1,0:T(8,128)(2,1)}), bf16[64,1,10,256]{3,2,1,0:T(8,128)(2,1)S(1)}, u32[]{:S(2)}, u32[]{:S(2)}) async-start(bf16[64,1,10,256]{3,2,1,0:T(8,128)(2,1)} %reshape.196), calls=%async_computation.2 | async-start | bytes 1048576 | tf_op jit(solution)/shard_map/all_to_all | solution.py:73
Sparse Core Ops, SparseCore 0:
  11.5 115.4 all-gather.7
  128.8 116.4 all-gather.3
  248.8 149.2 all-gather.5
where the time goes:
time: 443 us; the launch traced here: 442 us
  waiting for transfers between devices  330 us (74%)
  local copies, waits for them, and re-layouts  33.7 us (8%)
  starting transfers between devices  31.5 us (7%)
  matrix products  30.5 us (7%)
  between operations  13.9 us (3%)
    all_gather x1, waiting for transfers between devices, body(): gathered = lax.all_gather(tokens, 'fsdp', axis=1, tiled=True)  107 us
    all_gather x1, waiting for transfers between devices, body(): acc_strided = add_rows(lax.all_gather(w_strided, 'seq', axis=0, tiled=True))  101 us
    all_gather x1, waiting for transfers between devices, body(): acc_local = add_rows(lax.all_gather(w_local, 'seq', axis=0, tiled=True))  68.7 us
    all_to_all x1, waiting for transfers between devices, body(): lax.all_to_all(packed, 'seq', split_axis=1, concat_axis=0, tiled=True)  37.1 us
    dot_general x2, matrix products, add_rows(): jnp.dot(gathered, piece.reshape(rows, -1), preferred_element_type=jnp.flo...  22.4 us
    all_to_all x1, starting transfers between devices, body(): lax.all_to_all(marks, 'seq', split_axis=1, concat_axis=0, tiled=True)  15.6 us
    all_gather x1, local copies, waits for them, and re-layouts, body(): acc_local = add_rows(lax.all_gather(w_local, 'seq', axis=0, tiled=True))  15 us
    all_to_all x1, waiting for transfers between devices, body(): lax.all_to_all(result, 'seq', split_axis=0, concat_axis=1, tiled=True)  14.2 us
  transfers between devices with their start and end apart: 6, of which 5 were waited for; matrix products, arithmetic and copies ran while one was open for 7% of the time, Pallas kernels for 0%

commit v1 on v0

--- a/solution.py
+++ b/solution.py
@@ -3,6 +3,7 @@
 import jax.numpy as jnp
 from jax import lax
 from jax.sharding import PartitionSpec as P
+from jax.lax import all_to_all, axis_size
 
 HD = 128
 BLK = 128
@@ -44,7 +45,13 @@
         return jnp.dot(gathered, piece.reshape(rows, -1), preferred_element_type=jnp.float32)
 
     acc_local = add_rows(lax.all_gather(w_local, "seq", axis=0, tiled=True))
-    acc_strided = add_rows(lax.all_gather(w_strided, "seq", axis=0, tiled=True))
+
+    def connect_the_shelves(named_axis, page):
+        return jnp.concatenate(
+            all_to_all(jnp.stack([page] * axis_size(named_axis), axis=0), named_axis, 0, 0), axis=0
+        )
+
+    acc_strided = add_rows(connect_the_shelves("seq", w_strided))
     packed = acc_strided.astype(jnp.bfloat16).reshape(1, peers, per_peer, 3 * strided_cols)
     marks = valid.astype(jnp.bfloat16).reshape(1, peers, per_peer)
     strided_packed = lax.all_to_all(packed, "seq", split_axis=1, concat_axis=0, tiled=True)

time: 443 us -> 505 us (1.14)
  starting transfers between devices: 31.5 us -> 64.8 us
  local copies, waits for them, and re-layouts: 33.7 us -> 48 us
  waiting for transfers between devices: 330 us -> 344 us
    all_to_all x0 -> x1, waiting for transfers between devices: none -> 221 us  [connect_the_shelves(): all_to_all(jnp.stack([page] * axis_size(named_axis), axis=0), named_axis,...]
    all_gather x1, waiting for transfers between devices: 107 us -> 0.01 us  [body(): gathered = lax.all_gather(tokens, 'fsdp', axis=1, tiled=True)]
    all_gather x1 -> x0, waiting for transfers between devices: 101 us -> none  [body(): acc_strided = add_rows(lax.all_gather(w_strided, 'seq', axis=0, tiled=True))]
    all_to_all x1, starting transfers between devices: 11.4 us -> 39.1 us  [body(): lax.all_to_all(packed, 'seq', split_axis=1, concat_axis=0, tiled=True)]
    all_to_all x1, waiting for transfers between devices: 14.2 us -> 34.8 us  [body(): lax.all_to_all(result, 'seq', split_axis=0, concat_axis=1, tiled=True)]
    all_to_all x0 -> x1, starting transfers between devices: none -> 15.9 us  [connect_the_shelves(): all_to_all(jnp.stack([page] * axis_size(named_axis), axis=0), named_axis,...]
    all_to_all x1, starting transfers between devices: 15.6 us -> 4.17 us  [body(): lax.all_to_all(marks, 'seq', split_axis=1, concat_axis=0, tiled=True)]
    all_to_all x0 -> x1, local copies, waits for them, and re-layouts: none -> 11.3 us  [connect_the_shelves(): all_to_all(jnp.stack([page] * axis_size(named_axis), axis=0), named_axis,...]
  transfers between devices with their start and end apart: 6 -> 6, of which waited for: 5 -> 4; matrix products, arithmetic and copies ran while one was open for 7% -> 9% of each run, Pallas kernels for 0% -> 0%
where the time goes in v1:
time: 505 us; the launch traced here: 503 us
  waiting for transfers between devices  344 us (68%)
  starting transfers between devices  64.8 us (13%)
  local copies, waits for them, and re-layouts  48 us (10%)
  matrix products  30.5 us (6%)
  between operations  14.2 us (3%)
    all_to_all x1, waiting for transfers between devices, connect_the_shelves(): all_to_all(jnp.stack([page] * axis_size(named_axis), axis=0), named_axis,...  221 us
    all_gather x1, waiting for transfers between devices, body(): acc_local = add_rows(lax.all_gather(w_local, 'seq', axis=0, tiled=True))  59 us
    all_to_all x1, starting transfers between devices, body(): lax.all_to_all(packed, 'seq', split_axis=1, concat_axis=0, tiled=True)  39.1 us
    all_to_all x1, waiting for transfers between devices, body(): lax.all_to_all(result, 'seq', split_axis=0, concat_axis=1, tiled=True)  34.8 us
    all_to_all x1, waiting for transfers between devices, body(): lax.all_to_all(packed, 'seq', split_axis=1, concat_axis=0, tiled=True)  27.6 us
    dot_general x2, matrix products, add_rows(): jnp.dot(gathered, piece.reshape(rows, -1), preferred_element_type=jnp.flo...  22.4 us
    all_to_all x1, starting transfers between devices, connect_the_shelves(): all_to_all(jnp.stack([page] * axis_size(named_axis), axis=0), named_axis,...  15.9 us
    all_gather x1, local copies, waits for them, and re-layouts, body(): acc_local = add_rows(lax.all_gather(w_local, 'seq', axis=0, tiled=True))  15 us
  transfers between devices with their start and end apart: 6, of which 4 were waited for; matrix products, arithmetic and copies ran while one was open for 9% of the time, Pallas kernels for 0%

profile of v1, /device:TPU:1, one launch (start us, length us, event | category | flops | bytes accessed | tf_op | source)
XLA Modules:
  0.0 502.7 jit_solution(10350871059762677763)
XLA Ops:
  7.2 0.0 all-gather.3.cloned.1.call-start
  7.2 0.7 all-gather.3.cloned.1.call-update
  7.9 0.0 all-gather.5.cloned.1.call-start
  7.9 0.7 all-gather.5.cloned.1.call-update
  8.6 4.6 stack.2
  13.2 0.0 copy-start
  13.2 15.9 %all-to-all-start = ((bf16[64,80,3,256]{3,1,2,0:T(8,128)(2,1)}), bf16[64,80,3,256]{3,1,2,0:T(8,128)(2,1)}, u32[]{:S(2)}, u32[]{:S(2)}) async-start(bf16[64,80,3,256]{3,1,2,0:T(8,128)(2,1)} %stack.2), calls=%async_computation | async-start | bytes 15728640 | tf_op jit(solution)/shard_map/all_to_all | solution.py:51
  29.1 0.0 copy-done
  29.2 0.8 reshape.193
  30.0 221.1 %all-to-all-done = bf16[64,80,3,256]{3,1,2,0:T(8,128)(2,1)} async-done(((bf16[64,80,3,256]{3,1,2,0:T(8,128)(2,1)}), bf16[64,80,3,256]{3,1,2,0:T(8,128)(2,1)}, u32[]{:S(2)}, u32[]{:S(2)}) %all-to-all-start) | async-done | bytes 7864352 | tf_op jit(solution)/shard_map/all_to_all | solution.py:51
  251.0 4.2 all-to-all-start.2
  255.2 11.3 %copy.52 = bf16[64,80,3,256]{3,2,1,0:T(4,128)(2,1)} copy(bf16[64,80,3,256]{3,1,2,0:T(8,128)(2,1)} %all-to-all-done) | data formatting | bytes 15728640 | tf_op jit(solution)/shard_map/all_to_all | solution.py:51
  266.5 9.4 %copy.77 = bf16[640,8,3,256]{3,1,2,0:T(8,128)(2,1)} copy(bf16[640,8,3,256]{3,2,1,0:T(4,128)(2,1)} %bitcast.61) | data formatting | bytes 15728640
  275.9 0.0 all-gather.3.cloned.1.call-done
  275.9 9.6 %convolution_convert_fusion.1 = bf16[640,768]{1,0:T(8,128)(2,1)S(1)} fusion(bf16[640,5120]{1,0:T(8,128)(2,1)} %all-gather.3.cloned.1.call-done, bf16[5120,768]{1,0:T(8,128)(2,1)} %bitcast.63), kind=kOutput, calls=%fused_computation.17 | convolution fusion | flops 5033656320 | bytes 15400960 | tf_op jit(solution)/shard_map/dot_general | solution.py:45
  285.6 1.4 reshape.187
  287.0 0.0 all-to-all-done.2
  287.0 39.1 %all-to-all-start.1 = ((bf16[1,64,10,768]{3,2,0,1:T(8,128)(2,1)}), bf16[1,64,10,768]{3,2,0,1:T(8,128)(2,1)S(1)}, u32[]{:S(2)}, u32[]{:S(2)}) async-start(bf16[1,64,10,768]{3,2,0,1:T(8,128)(2,1)} %bitcast.7), calls=%async_computation.1 | async-start | bytes 3145728 | tf_op jit(solution)/shard_map/all_to_all | solution.py:57
  326.2 0.1 copy.57
  326.3 0.2 or_and_fusion
  326.5 27.6 %all-to-all-done.1 = bf16[1,64,10,768]{3,2,0,1:T(8,128)(2,1)S(1)} async-done(((bf16[1,64,10,768]{3,2,0,1:T(8,128)(2,1)}), bf16[1,64,10,768]{3,2,0,1:T(8,128)(2,1)S(1)}, u32[]{:S(2)}, u32[]{:S(2)}) %all-to-all-start.1) | async-done | bytes 983072 | tf_op jit(solution)/shard_map/all_to_all | solution.py:57
  354.0 0.6 reshape.192
  354.6 0.0 copy-start.1
  354.6 0.7 fusion.30
  355.3 0.3 fusion.14
  355.6 0.2 fusion.32
  355.8 0.3 fusion.15
  356.1 0.3 copy.70
  356.5 1.0 reshape.194
  357.5 5.5 %all-to-all-start.3 = ((bf16[64,1,10,256]{3,2,1,0:T(8,128)(2,1)}), bf16[64,1,10,256]{3,2,1,0:T(8,128)(2,1)S(1)}, u32[]{:S(2)}, u32[]{:S(2)}) async-start(bf16[64,1,10,256]{3,2,1,0:T(8,128)(2,1)} %reshape.194), calls=%async_computation.3 | async-start | bytes 1048576 | tf_op jit(solution)/shard_map/all_to_all | solution.py:80
  363.0 0.1 iota_compare_fusion.1
  363.1 0.0 copy-done.1
  363.1 0.1 broadcast_subtract_fusion
  363.2 0.9 fusion.10
  364.1 34.8 %all-to-all-done.3 = bf16[64,1,10,256]{3,2,1,0:T(8,128)(2,1)S(1)} async-done(((bf16[64,1,10,256]{3,2,1,0:T(8,128)(2,1)}), bf16[64,1,10,256]{3,2,1,0:T(8,128)(2,1)S(1)}, u32[]{:S(2)}, u32[]{:S(2)}) %all-to-all-start.3) | async-done | bytes 327712 | tf_op jit(solution)/shard_map/all_to_all | solution.py:80
  398.9 0.8 reshape.191
  399.7 59.0 %all-gather.5.cloned.1.call-done = bf16[5120,3,384]{2,0,1:T(8,128)(2,1)} async-done(((bf16[80,3,384]{2,0,1:T(8,128)(2,1)}), bf16[5120,3,384]{2,0,1:T(8,128)(2,1)}) %all-gather.5.cloned.1.call-update) | async-done | bytes 11796496 | tf_op jit(solution)/shard_map/all_gather | solution.py:47
  458.7 15.0 %copy.47 = bf16[5120,3,384]{0,2,1:T(8,128)(2,1)} copy(bf16[5120,3,384]{2,0,1:T(8,128)(2,1)} %all-gather.5.cloned.1.call-done) | data formatting | bytes 23592960 | tf_op jit(solution)/shard_map/all_gather | solution.py:47
  473.7 12.7 %convolution_convert_fusion = bf16[640,1152]{1,0:T(8,128)(2,1)S(1)} fusion(bf16[640,5120]{1,0:T(8,128)(2,1)} %all-gather.3.cloned.1.call-done, bf16[5120,1152]{0,1:T(8,128)(2,1)} %bitcast.62), kind=kOutput, calls=%fused_computation.5 | convolution fusion | flops 7550484480 | bytes 19824640 | tf_op jit(solution)/shard_map/dot_general | solution.py:45
  486.5 0.9 copy.48
  487.4 3.5 fusion.31
  490.9 4.0 fusion.12
  494.9 1.0 copy.63
  (5 shorter events, 0.1 us)
Async XLA Ops:
  7.2 268.8 %all-gather.3.cloned.1.call-start = ((), (), s32[]{:S(2)}) async-start(), calls=%async_computation.4 | async-start | bytes 8192000 | tf_op jit(solution)/shard_map/all_gather | solution.py:35
  7.9 450.8 %all-gather.5.cloned.1.call-start = ((), (), s32[]{:S(2)}) async-start(), calls=%async_computation.5 | async-start | bytes 11980800 | tf_op jit(solution)/shard_map/all_gather | solution.py:47
  13.2 15.9 %copy-start = (s32[1,640]{1,0:T(1,128)S(1)}, s32[1,640]{1,0:T(1,128)}, u32[]{:S(2)}) copy-start(s32[1,640]{1,0:T(1,128)} %param.8) | copy-start | bytes 7684
  13.2 237.8 %all-to-all-start = ((bf16[64,80,3,256]{3,1,2,0:T(8,128)(2,1)}), bf16[64,80,3,256]{3,1,2,0:T(8,128)(2,1)}, u32[]{:S(2)}, u32[]{:S(2)}) async-start(bf16[64,80,3,256]{3,1,2,0:T(8,128)(2,1)} %stack.2), calls=%async_computation | async-start | bytes 15728640 | tf_op jit(solution)/shard_map/all_to_all | solution.py:51
  251.0 36.0 %all-to-all-start.2 = ((bf16[1,64,10]{2,0,1:T(2,128)(2,1)}), bf16[1,64,10]{2,0,1:T(2,128)(2,1)S(1)}, u32[]{:S(2)}, u32[]{:S(2)}) async-start(bf16[1,64,10]{2,0,1:T(2,128)(2,1)} %reshape.193), calls=%async_computation.2 | async-start | bytes 65536 | tf_op jit(solution)/shard_map/all_to_all | solution.py:58
  287.0 67.0 %all-to-all-start.1 = ((bf16[1,64,10,768]{3,2,0,1:T(8,128)(2,1)}), bf16[1,64,10,768]{3,2,0,1:T(8,128)(2,1)S(1)}, u32[]{:S(2)}, u32[]{:S(2)}) async-start(bf16[1,64,10,768]{3,2,0,1:T(8,128)(2,1)} %bitcast.7), calls=%async_computation.1 | async-start | bytes 3145728 | tf_op jit(solution)/shard_map/all_to_all | solution.py:57
  354.6 8.5 %copy-start.1 = (s32[3]{0:T(128)S(1)}, s32[3]{0:T(128)}, u32[]{:S(2)}) copy-start(s32[3]{0:T(128)} %param.9) | copy-start | bytes 40
  357.5 41.4 %all-to-all-start.3 = ((bf16[64,1,10,256]{3,2,1,0:T(8,128)(2,1)}), bf16[64,1,10,256]{3,2,1,0:T(8,128)(2,1)S(1)}, u32[]{:S(2)}, u32[]{:S(2)}) async-start(bf16[64,1,10,256]{3,2,1,0:T(8,128)(2,1)} %reshape.194), calls=%async_computation.3 | async-start | bytes 1048576 | tf_op jit(solution)/shard_map/all_to_all | solution.py:80
Sparse Core Ops, SparseCore 0:
  9.8 264.1 all-gather.2
  277.5 181.2 all-gather.4
